TPU v7x, 32 devices: a whole 2x2x4 slice. The times are simulated.
32 devices in a mesh: seq: 16 (over z, x, core), head: 2 (over y).
Axes of the slice: x: 2, y: 2, z: 4, core: 2. Of those that a mesh axis runs over, the one named last changes fastest.
Arguments:
- queries: bfloat16 [4096, 4096], P(('seq', 'head')), may hold values from -130 to 130
- keys: bfloat16 [4096, 1024], P(('seq', 'head')), may hold values from -5 to 5
- values: bfloat16 [4096, 1024], P(('seq', 'head')), may hold values from -6 to 6
- vertical: int32 [8, 128], P('head'), may hold values from 0 to 4095, as said below
- slash: int32 [8, 64, 40], P('head'), may hold values from -1 to 59, as said below
Outputs:
- attended: bfloat16 [4096, 4096], P(('seq', 'head'))
Inputs may be any that keep to these rules, and one draw needn't show every extreme that they name: `vertical`: for each KV head the 128 entries are distinct token positions; the 256 tokens of one seq shard hold at most 15 of them, and for every head some seq shard holds exactly that many. Each KV head h has 40 distinct block offsets d[h, n], each at least 4, and some offset of every head equals 4; slash[h, b, n] = b - d[h, n] where that is not negative, else -1.
All inputs are finite; a program needn't handle non-finite values.
Results may differ from a plain program's by a relative error of at most 0.0052.
Values may be sent and summed in bfloat16 or wider, within the bound.
No kernel may reach another device: no remote copies, remote signals or barrier semaphores. Data moves between devices by JAX's collectives and lax.ppermute only.
A program may use at most 128 MiB of HBM per device.

v0:
```python
import math
import jax
import jax.numpy as jnp
from jax import lax
from jax.sharding import PartitionSpec as P

BLK = 64
NS = 40


def live_entries(lists):
    count = lists.shape[-1]
    earlier = jnp.arange(count)[:, None] > jnp.arange(count)[None, :]
    repeated = jnp.any(earlier & (lists[..., :, None] == lists[..., None, :]), axis=-1)
    return (lists >= 0) & jnp.logical_not(repeated)


def block_attention(
    query_part,
    diag_part,
    slash_part,
    slash_live,
    slash_list,
    vert_part,
    vert_where,
    block_ids,
    head_dim,
):
    scaling = 1.0 / math.sqrt(head_dim)
    width = query_part.shape[1]
    steps = query_part.shape[0]
    rows = query_part.shape[2]
    listed = slash_part.shape[1]
    positions = block_ids[:, None] * width + jnp.arange(width, dtype=jnp.int32)[None, :]
    first = (
        jnp.einsum(
            "gqrd,gkd->gqrk",
            query_part,
            diag_part[..., :head_dim],
            preferred_element_type=jnp.float32,
        )
        * scaling
    )
    causal = jnp.arange(width)[None, :] <= jnp.arange(width)[:, None]
    first = jnp.where(causal[None, :, None, :], first, -jnp.inf)
    second = (
        jnp.einsum(
            "gqrd,gnkd->gqrnk",
            query_part,
            slash_part[..., :head_dim],
            preferred_element_type=jnp.float32,
        )
        * scaling
    )
    second = jnp.where(slash_live[:, None, None, :, None], second, -jnp.inf)
    second = second.reshape(steps, width, rows, listed * width)
    third = (
        jnp.einsum(
            "gqrd,vd->gqrv", query_part, vert_part[:, :head_dim], preferred_element_type=jnp.float32
        )
        * scaling
    )
    vert_block = vert_where // width
    covered = (vert_block[None, :] == block_ids[:, None]) | jnp.any(
        slash_live[:, :, None] & (slash_list[:, :, None] == vert_block[None, None, :]), axis=1
    )
    visible = (vert_where[None, None, :] <= positions[:, :, None]) & jnp.logical_not(covered)[
        :, None, :
    ]
    third = jnp.where(visible[:, :, None, :], third, -jnp.inf)
    scores = jnp.concatenate([first, second, third], axis=-1)
    top = jnp.max(scores, axis=-1, keepdims=True)
    expo = jnp.exp(scores - top)
    total = jnp.sum(expo, axis=-1, keepdims=True)
    weights = (expo / total).astype(jnp.bfloat16)
    w_diag = weights[..., :width]
    w_slash = weights[..., width : width + listed * width].reshape(
        steps, width, rows, listed, width
    )
    w_vert = weights[..., width + listed * width :]
    out_diag = jnp.einsum(
        "gqrk,gkd->gqrd", w_diag, diag_part[..., head_dim:], preferred_element_type=jnp.float32
    )
    out_slash = jnp.einsum(
        "gqrnk,gnkd->gqrd", w_slash, slash_part[..., head_dim:], preferred_element_type=jnp.float32
    )
    out_vert = jnp.einsum(
        "gqrv,vd->gqrd", w_vert, vert_part[:, head_dim:], preferred_element_type=jnp.float32
    )
    return (out_diag + out_slash + out_vert).astype(jnp.bfloat16)


def make_step(own_rows, head_index, vert_head, vert_where, head_dim):

    def per_step(items):
        query_part, diag_part, slash_list, slash_live, sources, ident = items
        slash_part = own_rows[sources, :, head_index]
        return block_attention(
            query_part,
            diag_part,
            slash_part,
            slash_live,
            slash_list,
            vert_head,
            vert_where,
            ident,
            head_dim,
        )

    return per_step


def body(queries, keys, values, vertical, slash):
    query_rows, key_rows, value_rows = (
        lax.all_to_all(queries, "head", split_axis=1, concat_axis=0, tiled=True),
        lax.all_to_all(keys, "head", split_axis=1, concat_axis=0, tiled=True),
        lax.all_to_all(values, "head", split_axis=1, concat_axis=0, tiled=True),
    )
    shards = lax.axis_size("seq")
    seq_rank = lax.axis_index("seq")
    tok_count = key_rows.shape[0]
    local_heads = vertical.shape[0]
    head_dim = key_rows.shape[1] // local_heads
    group = query_rows.shape[1] // key_rows.shape[1]
    blocks_here = tok_count // BLK
    first_block = seq_rank * blocks_here
    paired = jnp.concatenate(
        [
            key_rows.reshape(tok_count, local_heads, head_dim),
            value_rows.reshape(tok_count, local_heads, head_dim),
        ],
        axis=2,
    )
    by_dest = slash.reshape(local_heads, shards, blocks_here * NS)
    own_ids = first_block + jnp.arange(blocks_here, dtype=jnp.int32)
    needed = jnp.any(by_dest[:, :, :, None] == own_ids[None, None, None, :], axis=2)
    needed = jnp.transpose(needed, (1, 2, 0))
    own_blocks = paired.reshape(blocks_here, BLK, local_heads, 2 * head_dim)
    outgoing = jnp.where(needed[:, :, None, :, None], own_blocks[None], jnp.zeros((), jnp.bfloat16))
    outgoing = outgoing.reshape(shards, tok_count, local_heads, 2 * head_dim)
    vert_shard = vertical // tok_count
    owned = vert_shard == seq_rank
    local_where = vertical - seq_rank * tok_count
    incoming = lax.all_to_all(outgoing, "seq", split_axis=0, concat_axis=0, tiled=True)
    token_iota = jnp.arange(tok_count)
    select = ((local_where[:, :, None] == token_iota[None, None, :]) & owned[:, :, None]).astype(
        jnp.bfloat16
    )
    partial_rows = jnp.einsum("hvt,thx->hvx", select, paired, preferred_element_type=jnp.float32)
    vert_part = lax.psum(partial_rows, "seq").astype(jnp.bfloat16)
    mine = lax.dynamic_slice_in_dim(slash, first_block, blocks_here, axis=1)
    live = live_entries(mine)
    source_block = jnp.where(live, mine, 0)
    step_blocks = math.gcd(blocks_here, 2)
    steps_count = blocks_here // step_blocks
    block_ids = (first_block + jnp.arange(blocks_here, dtype=jnp.int32)).reshape(
        steps_count, step_blocks
    )
    query_all = query_rows.reshape(steps_count, step_blocks, BLK, local_heads, group, head_dim)
    all_blocks = incoming.reshape(shards * blocks_here, BLK, local_heads, 2 * head_dim)
    results = []
    for head_index in range(local_heads):
        per_step = make_step(
            all_blocks, head_index, vert_part[head_index], vertical[head_index], head_dim
        )
        diag_all = paired[:, head_index].reshape(steps_count, step_blocks, BLK, 2 * head_dim)
        lists = mine[head_index].reshape(steps_count, step_blocks, NS)
        lives = live[head_index].reshape(steps_count, step_blocks, NS)
        sources = source_block[head_index].reshape(steps_count, step_blocks, NS)
        outputs = lax.map(
            per_step, (query_all[:, :, :, head_index], diag_all, lists, lives, sources, block_ids)
        )
        results.append(outputs)
    stacked = jnp.stack(results, axis=3).reshape(tok_count, local_heads * group * head_dim)
    return lax.all_to_all(stacked, "head", split_axis=0, concat_axis=1, tiled=True)


def solution(mesh):
    in_specs = (
        P(("seq", "head"), None),
        P(("seq", "head"), None),
        P(("seq", "head"), None),
        P("head", None),
        P("head", None, None),
    )
    out_specs = P(("seq", "head"), None)
    return jax.shard_map(body, mesh=mesh, in_specs=in_specs, out_specs=out_specs, check_vma=False)
```

profile of v0, /device:TPU:11, one launch (start us, length us, event | category | flops | bytes accessed | tf_op | source)
XLA Modules:
  0.0 733.0 jit_solution(8951616375855945567)
XLA Ops:
  34.7 8.3 %all-to-all-start.3 = ((bf16[16,256,4,256]{3,1,2,0:T(8,128)(2,1)}), bf16[16,256,4,256]{3,1,2,0:T(8,128)(2,1)}, u32[]{:S(2)}, u32[]{:S(2)}) async-start(bf16[16,256,4,256]{3,1,2,0:T(8,128)(2,1)} %broadcast_select_fusion), calls=%async_computation.3 | async-start | bytes 16777216 | tf_op jit(solution)/shard_map/all_to_all | solution.py:144
  48.8 219.5 %all-reduce.5 = bf16[4,128,256]{2,1,0:T(8,128)(2,1)S(1)} all-reduce(f32[4,128,256]{2,1,0:T(8,128)S(1)} %fusion.118), channel_id=1, replica_groups=mesh['seq'=16,'head'=2] {'seq'}, use_global_device_ids=true, to_apply=%region_2.3 | all-reduce | flops 131072 | bytes 786432 | tf_op jit(solution)/shard_map/psum | solution.py:150
  271.7 7.7 %copy.163 = bf16[16,256,4,256]{3,1,0,2:T(8,128)(2,1)} copy(bf16[16,256,4,256]{3,1,2,0:T(8,128)(2,1)} %all-to-all-done.3) | data formatting | bytes 16777216 | tf_op jit(solution)/shard_map/all_to_all | solution.py:144
  279.4 8.3 %copy.165 = bf16[64,64,4,256]{3,1,2,0:T(8,128)(2,1)} copy(bf16[64,64,4,256]{3,1,0,2:T(8,128)(2,1)} %bitcast.710) | data formatting | bytes 16777216 | tf_op jit(solution)/shard_map/while | solution.py:170
  288.5 107.5 %while.52 = (s32[]{:T(128)}, bf16[2,2,64,4,128]{4,2,3,1,0:T(8,128)(2,1)}, bf16[2,2,64,4,128]{4,3,2,1,0:T(4,128)(2,1)}, bf16[2,2,64,256]{3,2,1,0:T(8,128)(2,1)}, ...) while((s32[]{:T(128)}, ...), condition=%wide.region_9.10_spmd, body=%wide.region_3.9_spmd.sunk | while | flops 732959872 | bytes 101075352 | solution.py:170
  302.9 9.2 %copy.334 = f32[2,64,4,2560]{3,1,2,0:T(8,128)} copy(f32[2,64,4,2560]{1,3,2,0:T(8,128)} %bitcast.698) | data formatting | bytes 10485760 | tf_op jit(solution)/shard_map/while/body/eval_jaxpr/reshape | solution.py:56
  328.7 7.6 %reshape.1116 = bf16[2,64,4,40,64]{4,3,1,2,0:T(8,128)(2,1)} reshape(bf16[2,64,4,2560]{3,1,2,0:T(8,128)(2,1)} %slice.620) | data formatting | bytes 5242880 | tf_op jit(solution)/shard_map/while/body/eval_jaxpr/reshape | solution.py:77
  356.6 9.2 %copy.334 = f32[2,64,4,2560]{3,1,2,0:T(8,128)} copy(f32[2,64,4,2560]{1,3,2,0:T(8,128)} %bitcast.698) | data formatting | bytes 10485760 | tf_op jit(solution)/shard_map/while/body/eval_jaxpr/reshape | solution.py:56
  382.4 7.6 %reshape.1116 = bf16[2,64,4,40,64]{4,3,1,2,0:T(8,128)(2,1)} reshape(bf16[2,64,4,2560]{3,1,2,0:T(8,128)(2,1)} %slice.620) | data formatting | bytes 5242880 | tf_op jit(solution)/shard_map/while/body/eval_jaxpr/reshape | solution.py:77
  396.7 103.0 %while.53 = (s32[]{:T(128)}, bf16[2,2,64,4,128]{4,2,3,1,0:T(8,128)(2,1)}, bf16[2,2,64,4,128]{4,3,2,1,0:T(4,128)(2,1)S(1)}, bf16[2,2,64,256]{3,2,1,0:T(8,128)(2,1...) while((s32[]{:T(128)}, ...), condition=%wide.region_16.17_spmd, body=%wide.region_10.16_spmd.sunk | while | flops 732960000 | bytes 100545856 | solution.py:170
  410.0 9.1 %copy.339 = f32[2,64,4,2560]{3,1,2,0:T(8,128)} copy(f32[2,64,4,2560]{1,3,2,0:T(8,128)} %bitcast.699) | data formatting | bytes 10485760 | tf_op jit(solution)/shard_map/while/body/eval_jaxpr/reshape | solution.py:56
  435.7 7.6 %reshape.1120 = bf16[2,64,4,40,64]{4,3,1,2,0:T(8,128)(2,1)} reshape(bf16[2,64,4,2560]{3,1,2,0:T(8,128)(2,1)} %slice.629) | data formatting | bytes 5242880 | tf_op jit(solution)/shard_map/while/body/eval_jaxpr/reshape | solution.py:77
  461.2 9.1 %copy.339 = f32[2,64,4,2560]{3,1,2,0:T(8,128)} copy(f32[2,64,4,2560]{1,3,2,0:T(8,128)} %bitcast.699) | data formatting | bytes 10485760 | tf_op jit(solution)/shard_map/while/body/eval_jaxpr/reshape | solution.py:56
  500.5 107.4 %while.54 = (s32[]{:T(128)}, bf16[2,2,64,4,128]{4,2,3,1,0:T(8,128)(2,1)}, bf16[2,2,64,4,128]{4,3,2,1,0:T(4,128)(2,1)}, bf16[2,2,64,256]{3,2,1,0:T(8,128)(2,1)}, ...) while((s32[]{:T(128)}, ...), condition=%wide.region_23.24_spmd, body=%wide.region_17.23_spmd.sunk | while | flops 732960000 | bytes 101332344 | solution.py:170
  515.7 9.2 %copy.344 = f32[2,64,4,2560]{3,1,2,0:T(8,128)} copy(f32[2,64,4,2560]{1,3,2,0:T(8,128)} %bitcast.700) | data formatting | bytes 10485760 | tf_op jit(solution)/shard_map/while/body/eval_jaxpr/reshape | solution.py:56
  541.6 7.6 %reshape.1124 = bf16[2,64,4,40,64]{4,3,1,2,0:T(8,128)(2,1)} reshape(bf16[2,64,4,2560]{3,1,2,0:T(8,128)(2,1)} %slice.638) | data formatting | bytes 5242880 | tf_op jit(solution)/shard_map/while/body/eval_jaxpr/reshape | solution.py:77
  569.3 9.2 %copy.344 = f32[2,64,4,2560]{3,1,2,0:T(8,128)} copy(f32[2,64,4,2560]{1,3,2,0:T(8,128)} %bitcast.700) | data formatting | bytes 10485760 | tf_op jit(solution)/shard_map/while/body/eval_jaxpr/reshape | solution.py:56
  595.1 7.6 %reshape.1124 = bf16[2,64,4,40,64]{4,3,1,2,0:T(8,128)(2,1)} reshape(bf16[2,64,4,2560]{3,1,2,0:T(8,128)(2,1)} %slice.638) | data formatting | bytes 5242880 | tf_op jit(solution)/shard_map/while/body/eval_jaxpr/reshape | solution.py:77
  608.7 102.8 %while.55 = (s32[]{:T(128)}, bf16[2,2,64,4,128]{4,2,3,1,0:T(8,128)(2,1)}, bf16[2,2,64,4,128]{4,3,2,1,0:T(4,128)(2,1)S(1)}, bf16[2,2,64,256]{3,2,1,0:T(8,128)(2,1...) while((s32[]{:T(128)}, ...), condition=%wide.region_30.31_spmd, body=%wide.region_24.30_spmd.sunk | while | flops 732960000 | bytes 100545856 | solution.py:170
  621.6 9.2 %copy.349 = f32[2,64,4,2560]{3,1,2,0:T(8,128)} copy(f32[2,64,4,2560]{1,3,2,0:T(8,128)} %bitcast.701) | data formatting | bytes 10485760 | tf_op jit(solution)/shard_map/while/body/eval_jaxpr/reshape | solution.py:56
  647.4 7.6 %reshape.1128 = bf16[2,64,4,40,64]{4,3,1,2,0:T(8,128)(2,1)} reshape(bf16[2,64,4,2560]{3,1,2,0:T(8,128)(2,1)} %slice.647) | data formatting | bytes 5242880 | tf_op jit(solution)/shard_map/while/body/eval_jaxpr/reshape | solution.py:77
  672.9 9.2 %copy.349 = f32[2,64,4,2560]{3,1,2,0:T(8,128)} copy(f32[2,64,4,2560]{1,3,2,0:T(8,128)} %bitcast.701) | data formatting | bytes 10485760 | tf_op jit(solution)/shard_map/while/body/eval_jaxpr/reshape | solution.py:56
  698.7 7.6 %reshape.1128 = bf16[2,64,4,40,64]{4,3,1,2,0:T(8,128)(2,1)} reshape(bf16[2,64,4,2560]{3,1,2,0:T(8,128)(2,1)} %slice.647) | data formatting | bytes 5242880 | tf_op jit(solution)/shard_map/while/body/eval_jaxpr/reshape | solution.py:77
  714.4 16.4 %all_to_all.72 = bf16[2,128,2048]{2,1,0:T(8,128)(2,1)S(1)} all-to-all(bf16[2,128,2048]{2,1,0:T(8,128)(2,1)S(1)} %all_to_all.63), channel_id=1, replica_groups=mesh['seq'=16,'head'=2] {'head'}, dimensions={0} | all-to-all | bytes 2097152 | tf_op jit(solution)/shard_map/all_to_all | solution.py:175
  (316 shorter events, 344.3 us)
Async XLA Ops:
  1.7 9.4 %all-to-all-start.1 = ((bf16[128,2,512]{2,0,1:T(8,128)(2,1)}), bf16[128,2,512]{2,0,1:T(8,128)(2,1)S(1)}, u32[]{:S(2)}, u32[]{:S(2)}) async-start(bf16[128,2,512]{2,0,1:T(8,128)(2,1)} %bitcast.489), calls=%async_computation.1 | async-start | bytes 524288 | tf_op jit(solution)/shard_map/all_to_all | solution.py:116
  11.0 8.0 %all-to-all-start.2 = ((bf16[128,2,512]{2,0,1:T(8,128)(2,1)}), bf16[128,2,512]{2,0,1:T(8,128)(2,1)S(1)}, u32[]{:S(2)}, u32[]{:S(2)}) async-start(bf16[128,2,512]{2,0,1:T(8,128)(2,1)} %bitcast.488), calls=%async_computation.2 | async-start | bytes 524288 | tf_op jit(solution)/shard_map/all_to_all | solution.py:117
  19.0 15.7 %all-to-all-start = ((bf16[128,2,2048]{2,0,1:T(8,128)(2,1)}), bf16[128,2,2048]{2,0,1:T(8,128)(2,1)S(1)}, u32[]{:S(2)}, u32[]{:S(2)}) async-start(bf16[128,2,2048]{2,0,1:T(8,128)(2,1)} %bitcast.487), calls=%async_computation | async-start | bytes 2097152 | tf_op jit(solution)/shard_map/all_to_all | solution.py:115
  28.5 18.0 %copy-start.14 = (s32[4,128]{1,0:T(4,128)S(1)}, s32[4,128]{1,0:T(4,128)}, u32[]{:S(2)}) copy-start(s32[4,128]{1,0:T(4,128)} %param.16) | copy-start | bytes 6148
  34.7 237.0 %all-to-all-start.3 = ((bf16[16,256,4,256]{3,1,2,0:T(8,128)(2,1)}), bf16[16,256,4,256]{3,1,2,0:T(8,128)(2,1)}, u32[]{:S(2)}, u32[]{:S(2)}) async-start(bf16[16,256,4,256]{3,1,2,0:T(8,128)(2,1)} %broadcast_select_fusion), calls=%async_computation.3 | async-start | bytes 16777216 | tf_op jit(solution)/shard_map/all_to_all | solution.py:144
  298.0 4.9 copy-start.4
  302.9 9.2 %copy-start.11 = (bf16[2,2,64,256]{3,2,1,0:T(8,128)(2,1)S(1)}, bf16[2,2,64,256]{3,2,1,0:T(8,128)(2,1)}, u32[]{:S(2)}) copy-start(bf16[2,2,64,256]{3,2,1,0:T(8,128)(2,1)} %get-tuple-element.1995) | copy-start | bytes 393220 | tf_op jit(solution)/shard_map/while
  336.3 5.9 copy-start.17
  351.6 4.9 copy-start.4
  356.6 9.2 %copy-start.11 = (bf16[2,2,64,256]{3,2,1,0:T(8,128)(2,1)S(1)}, bf16[2,2,64,256]{3,2,1,0:T(8,128)(2,1)}, u32[]{:S(2)}) copy-start(bf16[2,2,64,256]{3,2,1,0:T(8,128)(2,1)} %get-tuple-element.1995) | copy-start | bytes 393220 | tf_op jit(solution)/shard_map/while
  389.9 6.0 copy-start.17
  405.0 4.9 copy-start.5
  456.3 4.9 copy-start.5
  500.5 108.2 %copy-start.8 = (bf16[2,2,64,4,128]{4,3,2,1,0:T(4,128)(2,1)S(1)}, bf16[2,2,64,4,128]{4,3,2,1,0:T(4,128)(2,1)}, u32[]{:S(2)}) copy-start(bf16[2,2,64,4,128]{4,3,2,1,0:T(4,128)(2,1)} %get-tuple-element.1807) | copy-start | bytes 786436
  500.5 108.2 %copy-start.9 = (bf16[256,1,256]{2,0,1:T(8,128)(2,1)S(1)}, bf16[256,1,256]{2,0,1:T(8,128)(2,1)}, u32[]{:S(2)}) copy-start(bf16[256,1,256]{2,0,1:T(8,128)(2,1)} %get-tuple-element.1294) | copy-start | bytes 393220
  500.5 108.2 %copy-start.12 = (bf16[128,256]{1,0:T(8,128)(2,1)S(1)}, bf16[128,256]{1,0:T(8,128)(2,1)}, u32[]{:S(2)}) copy-start(bf16[128,256]{1,0:T(8,128)(2,1)} %get-tuple-element.1820) | copy-start | bytes 196612
  500.5 108.2 %copy-start.15 = (s32[1,4,40]{2,1,0:T(4,128)S(1)}, s32[1,4,40]{2,1,0:T(4,128)}, u32[]{:S(2)}) copy-start(s32[1,4,40]{2,1,0:T(4,128)} %get-tuple-element.1302) | copy-start | bytes 1924
  510.8 4.9 copy-start.6
  515.7 9.2 %copy-start.10 = (bf16[2,2,64,256]{3,2,1,0:T(8,128)(2,1)S(1)}, bf16[2,2,64,256]{3,2,1,0:T(8,128)(2,1)}, u32[]{:S(2)}) copy-start(bf16[2,2,64,256]{3,2,1,0:T(8,128)(2,1)} %get-tuple-element.1893) | copy-start | bytes 393220 | tf_op jit(solution)/shard_map/while
  549.1 4.3 copy-start.13
  564.4 4.9 copy-start.6
  569.3 9.2 %copy-start.10 = (bf16[2,2,64,256]{3,2,1,0:T(8,128)(2,1)S(1)}, bf16[2,2,64,256]{3,2,1,0:T(8,128)(2,1)}, u32[]{:S(2)}) copy-start(bf16[2,2,64,256]{3,2,1,0:T(8,128)(2,1)} %get-tuple-element.1893) | copy-start | bytes 393220 | tf_op jit(solution)/shard_map/while
  616.7 4.9 copy-start.7
  668.0 4.9 copy-start.7
  (11 other events, 40.2 us)
where the time goes:
time: 741 us; the launch traced here: 733 us
  local copies, waits for them, and re-layouts  306 us (41%)
  blocking collectives  236 us (32%)
  matrix products  90.4 us (12%)
  other arithmetic  69.6 us (9%)
  starting transfers between devices  18.8 us (3%)
  waiting for transfers between devices  10.6 us (1%)
    psum x1, blocking collectives, body(): vert_part = lax.psum(partial_rows, 'seq').astype(jnp.bfloat16)  219 us
    reshape x8, local copies, waits for them, and re-layouts, block_attention(): second = second.reshape(steps, width, rows, listed * width)  73.5 us
    reshape x8, local copies, waits for them, and re-layouts, block_attention(): weights[..., width:width + listed * width]  60.4 us
    concatenate x8, local copies, waits for them, and re-layouts, block_attention(): scores = jnp.concatenate([first, second, third], axis=-1)  57.8 us
    dot_general x8, matrix products, block_attention(): jnp.einsum('gqrd,gnkd->gqrnk', query_part, slash_part[..., :head_dim], pr...  39.2 us
    gather x8, local copies, waits for them, and re-layouts, per_step(): slash_part = own_rows[sources, :, head_index]  34.6 us
    dot_general x8, matrix products, block_attention(): jnp.einsum('gqrnk,gnkd->gqrd', w_slash, slash_part[..., head_dim:], prefe...  33.1 us
    reduce_sum x8, other arithmetic, block_attention(): total = jnp.sum(expo, axis=-1, keepdims=True)  29.5 us
  transfers between devices with their start and end apart: 4, of which 2 were waited for; matrix products, arithmetic and copies ran while one was open for 3% of the time, Pallas kernels for 0%

commit v1 on v0

--- a/solution.py
+++ b/solution.py
@@ -147,7 +147,7 @@
         jnp.bfloat16
     )
     partial_rows = jnp.einsum("hvt,thx->hvx", select, paired, preferred_element_type=jnp.float32)
-    vert_part = lax.psum(partial_rows, "seq").astype(jnp.bfloat16)
+    vert_part = jnp.sum(lax.all_gather(partial_rows, "seq"), axis=0).astype(jnp.bfloat16)
     mine = lax.dynamic_slice_in_dim(slash, first_block, blocks_here, axis=1)
     live = live_entries(mine)
     source_block = jnp.where(live, mine, 0)

time: 741 us -> 764 us (1.031)
  waiting for transfers between devices: 10.6 us -> 234 us
  blocking collectives: 236 us -> 16 us
  between operations: 0.43 us -> 13.8 us
    all_to_all x1, waiting for transfers between devices: 0.01 us -> 223 us  [body(): lax.all_to_all(outgoing, 'seq', split_axis=0, concat_axis=0, tiled=True)]
    psum x1 -> x0, blocking collectives: 219 us -> none  [body(): vert_part = lax.psum(partial_rows, 'seq').astype(jnp.bfloat16)]
  transfers between devices with their start and end apart: 4 -> 5, of which waited for: 2 -> 3; matrix products, arithmetic and copies ran while one was open for 3% -> 5% of each run, Pallas kernels for 0% -> 0%
where the time goes in v1:
time: 764 us; the launch traced here: 756 us
  local copies, waits for them, and re-layouts  305 us (40%)
  waiting for transfers between devices  234 us (31%)
  matrix products  91.1 us (12%)
  other arithmetic  74.9 us (10%)
  starting transfers between devices  18.9 us (2%)
  blocking collectives  16 us (2%)
  between operations  13.8 us (2%)
    all_to_all x1, waiting for transfers between devices, body(): lax.all_to_all(outgoing, 'seq', split_axis=0, concat_axis=0, tiled=True)  223 us
    reshape x8, local copies, waits for them, and re-layouts, block_attention(): second = second.reshape(steps, width, rows, listed * width)  73 us
    reshape x8, local copies, waits for them, and re-layouts, block_attention(): weights[..., width:width + listed * width]  60.4 us
    concatenate x8, local copies, waits for them, and re-layouts, block_attention(): scores = jnp.concatenate([first, second, third], axis=-1)  57.7 us
    dot_general x8, matrix products, block_attention(): jnp.einsum('gqrd,gnkd->gqrnk', query_part, slash_part[..., :head_dim], pr...  39.1 us
    gather x8, local copies, waits for them, and re-layouts, per_step(): slash_part = own_rows[sources, :, head_index]  34.6 us
    dot_general x8, matrix products, block_attention(): jnp.einsum('gqrnk,gnkd->gqrd', w_slash, slash_part[..., head_dim:], prefe...  33.1 us
    reduce_sum x8, other arithmetic, block_attention(): total = jnp.sum(expo, axis=-1, keepdims=True)  29.5 us
  transfers between devices with their start and end apart: 5, of which 3 were waited for; matrix products, arithmetic and copies ran while one was open for 5% of the time, Pallas kernels for 0%

profile of v1, /device:TPU:11, one launch (start us, length us, event | category | flops | bytes accessed | tf_op | source)
XLA Modules:
  0.0 755.5 jit_solution(11178071733857756373)
XLA Ops:
  42.6 8.3 %all-to-all-start.3 = ((bf16[16,256,4,256]{3,1,2,0:T(8,128)(2,1)}), bf16[16,256,4,256]{3,1,2,0:T(8,128)(2,1)}, u32[]{:S(2)}, u32[]{:S(2)}) async-start(bf16[16,256,4,256]{3,1,2,0:T(8,128)(2,1)} %broadcast_select_fusion), calls=%async_computation.3 | async-start | bytes 16777216 | tf_op jit(solution)/shard_map/all_to_all | solution.py:144
  60.5 223.4 %all-to-all-done.3 = bf16[16,256,4,256]{3,1,2,0:T(8,128)(2,1)} async-done(((bf16[16,256,4,256]{3,1,2,0:T(8,128)(2,1)}), bf16[16,256,4,256]{3,1,2,0:T(8,128)(2,1)}, u32[]{:S(2)}, u32[]{:S(2)}) %all-to-all-start.3) | async-done | bytes 8388640 | tf_op jit(solution)/shard_map/all_to_all | solution.py:144
  283.8 7.7 %copy.163 = bf16[16,256,4,256]{3,1,0,2:T(8,128)(2,1)} copy(bf16[16,256,4,256]{3,1,2,0:T(8,128)(2,1)} %all-to-all-done.3) | data formatting | bytes 16777216 | tf_op jit(solution)/shard_map/all_to_all | solution.py:144
  291.6 8.3 %copy.165 = bf16[64,64,4,256]{3,1,2,0:T(8,128)(2,1)} copy(bf16[64,64,4,256]{3,1,0,2:T(8,128)(2,1)} %bitcast.711) | data formatting | bytes 16777216 | tf_op jit(solution)/shard_map/while | solution.py:170
  305.3 107.0 %while.52 = (s32[]{:T(128)}, bf16[2,2,64,4,128]{4,2,3,1,0:T(8,128)(2,1)}, bf16[2,2,64,4,128]{4,3,2,1,0:T(4,128)(2,1)}, bf16[2,2,64,256]{3,2,1,0:T(8,128)(2,1)}, ...) while((s32[]{:T(128)}, ...), condition=%wide.region_9.10_spmd, body=%wide.region_3.9_spmd.sunk | while | flops 732959872 | bytes 101075352 | solution.py:170
  319.5 9.1 %copy.334 = f32[2,64,4,2560]{3,1,2,0:T(8,128)} copy(f32[2,64,4,2560]{1,3,2,0:T(8,128)} %bitcast.699) | data formatting | bytes 10485760 | tf_op jit(solution)/shard_map/while/body/eval_jaxpr/reshape | solution.py:56
  345.3 7.6 %reshape.1117 = bf16[2,64,4,40,64]{4,3,1,2,0:T(8,128)(2,1)} reshape(bf16[2,64,4,2560]{3,1,2,0:T(8,128)(2,1)} %slice.620) | data formatting | bytes 5242880 | tf_op jit(solution)/shard_map/while/body/eval_jaxpr/reshape | solution.py:77
  373.0 9.1 %copy.334 = f32[2,64,4,2560]{3,1,2,0:T(8,128)} copy(f32[2,64,4,2560]{1,3,2,0:T(8,128)} %bitcast.699) | data formatting | bytes 10485760 | tf_op jit(solution)/shard_map/while/body/eval_jaxpr/reshape | solution.py:56
  398.8 7.6 %reshape.1117 = bf16[2,64,4,40,64]{4,3,1,2,0:T(8,128)(2,1)} reshape(bf16[2,64,4,2560]{3,1,2,0:T(8,128)(2,1)} %slice.620) | data formatting | bytes 5242880 | tf_op jit(solution)/shard_map/while/body/eval_jaxpr/reshape | solution.py:77
  413.1 103.0 %while.53 = (s32[]{:T(128)}, bf16[2,2,64,4,128]{4,2,3,1,0:T(8,128)(2,1)}, bf16[2,2,64,4,128]{4,3,2,1,0:T(4,128)(2,1)S(1)}, bf16[2,2,64,256]{3,2,1,0:T(8,128)(2,1...) while((s32[]{:T(128)}, ...), condition=%wide.region_16.17_spmd, body=%wide.region_10.16_spmd.sunk | while | flops 732960000 | bytes 100545856 | solution.py:170
  426.3 9.1 %copy.339 = f32[2,64,4,2560]{3,1,2,0:T(8,128)} copy(f32[2,64,4,2560]{1,3,2,0:T(8,128)} %bitcast.700) | data formatting | bytes 10485760 | tf_op jit(solution)/shard_map/while/body/eval_jaxpr/reshape | solution.py:56
  452.1 7.6 reshape.1121
  477.6 9.1 %copy.339 = f32[2,64,4,2560]{3,1,2,0:T(8,128)} copy(f32[2,64,4,2560]{1,3,2,0:T(8,128)} %bitcast.700) | data formatting | bytes 10485760 | tf_op jit(solution)/shard_map/while/body/eval_jaxpr/reshape | solution.py:56
  503.3 7.6 reshape.1121
  516.8 107.4 %while.54 = (s32[]{:T(128)}, bf16[2,2,64,4,128]{4,2,3,1,0:T(8,128)(2,1)}, bf16[2,2,64,4,128]{4,3,2,1,0:T(4,128)(2,1)}, bf16[2,2,64,256]{3,2,1,0:T(8,128)(2,1)}, ...) while((s32[]{:T(128)}, ...), condition=%wide.region_23.24_spmd, body=%wide.region_17.23_spmd.sunk | while | flops 732960000 | bytes 101332344 | solution.py:170
  532.1 9.1 %copy.344 = f32[2,64,4,2560]{3,1,2,0:T(8,128)} copy(f32[2,64,4,2560]{1,3,2,0:T(8,128)} %bitcast.701) | data formatting | bytes 10485760 | tf_op jit(solution)/shard_map/while/body/eval_jaxpr/reshape | solution.py:56
  557.8 7.5 reshape.1125
  585.6 9.1 %copy.344 = f32[2,64,4,2560]{3,1,2,0:T(8,128)} copy(f32[2,64,4,2560]{1,3,2,0:T(8,128)} %bitcast.701) | data formatting | bytes 10485760 | tf_op jit(solution)/shard_map/while/body/eval_jaxpr/reshape | solution.py:56
  611.4 7.5 reshape.1125
  624.9 102.6 %while.55 = (s32[]{:T(128)}, bf16[2,2,64,4,128]{4,2,3,1,0:T(8,128)(2,1)}, bf16[2,2,64,4,128]{4,3,2,1,0:T(4,128)(2,1)S(1)}, bf16[2,2,64,256]{3,2,1,0:T(8,128)(2,1...) while((s32[]{:T(128)}, ...), condition=%wide.region_30.31_spmd, body=%wide.region_24.30_spmd.sunk | while | flops 732960000 | bytes 100545856 | solution.py:170
  637.9 9.1 %copy.349 = f32[2,64,4,2560]{3,1,2,0:T(8,128)} copy(f32[2,64,4,2560]{1,3,2,0:T(8,128)} %bitcast.702) | data formatting | bytes 10485760 | tf_op jit(solution)/shard_map/while/body/eval_jaxpr/reshape | solution.py:56
  663.6 7.5 reshape.1129
  689.1 9.1 %copy.349 = f32[2,64,4,2560]{3,1,2,0:T(8,128)} copy(f32[2,64,4,2560]{1,3,2,0:T(8,128)} %bitcast.702) | data formatting | bytes 10485760 | tf_op jit(solution)/shard_map/while/body/eval_jaxpr/reshape | solution.py:56
  730.5 16.0 %all_to_all.72 = bf16[2,128,2048]{2,1,0:T(8,128)(2,1)S(1)} all-to-all(bf16[2,128,2048]{2,1,0:T(8,128)(2,1)S(1)} %all_to_all.63), channel_id=1, replica_groups=mesh['seq'=16,'head'=2] {'head'}, dimensions={0} | all-to-all | bytes 2097152 | tf_op jit(solution)/shard_map/all_to_all | solution.py:175
  (319 shorter events, 350.5 us)
Async XLA Ops:
  8.2 10.7 %all-to-all-start.1 = ((bf16[128,2,512]{2,0,1:T(8,128)(2,1)}), bf16[128,2,512]{2,0,1:T(8,128)(2,1)S(1)}, u32[]{:S(2)}, u32[]{:S(2)}) async-start(bf16[128,2,512]{2,0,1:T(8,128)(2,1)} %bitcast.490), calls=%async_computation.1 | async-start | bytes 524288 | tf_op jit(solution)/shard_map/all_to_all | solution.py:116
  18.9 8.0 %all-to-all-start.2 = ((bf16[128,2,512]{2,0,1:T(8,128)(2,1)}), bf16[128,2,512]{2,0,1:T(8,128)(2,1)S(1)}, u32[]{:S(2)}, u32[]{:S(2)}) async-start(bf16[128,2,512]{2,0,1:T(8,128)(2,1)} %bitcast.489), calls=%async_computation.2 | async-start | bytes 524288 | tf_op jit(solution)/shard_map/all_to_all | solution.py:117
  26.9 15.7 %all-to-all-start = ((bf16[128,2,2048]{2,0,1:T(8,128)(2,1)}), bf16[128,2,2048]{2,0,1:T(8,128)(2,1)S(1)}, u32[]{:S(2)}, u32[]{:S(2)}) async-start(bf16[128,2,2048]{2,0,1:T(8,128)(2,1)} %bitcast.488), calls=%async_computation | async-start | bytes 2097152 | tf_op jit(solution)/shard_map/all_to_all | solution.py:115
  36.5 19.2 %copy-start.14 = (s32[4,128]{1,0:T(4,128)S(1)}, s32[4,128]{1,0:T(4,128)}, u32[]{:S(2)}) copy-start(s32[4,128]{1,0:T(4,128)} %param.16) | copy-start | bytes 6148
  42.6 241.3 %all-to-all-start.3 = ((bf16[16,256,4,256]{3,1,2,0:T(8,128)(2,1)}), bf16[16,256,4,256]{3,1,2,0:T(8,128)(2,1)}, u32[]{:S(2)}, u32[]{:S(2)}) async-start(bf16[16,256,4,256]{3,1,2,0:T(8,128)(2,1)} %broadcast_select_fusion), calls=%async_computation.3 | async-start | bytes 16777216 | tf_op jit(solution)/shard_map/all_to_all | solution.py:144
  50.9 248.9 %all-gather.3.cloned.1.call-start = ((), (), s32[]{:S(2)}) async-start(), calls=%async_computation.5 | async-start | bytes 8912896 | tf_op jit(solution)/shard_map/all_gather | solution.py:150
  314.6 4.9 copy-start.4
  319.5 9.1 %copy-start.11 = (bf16[2,2,64,256]{3,2,1,0:T(8,128)(2,1)S(1)}, bf16[2,2,64,256]{3,2,1,0:T(8,128)(2,1)}, u32[]{:S(2)}) copy-start(bf16[2,2,64,256]{3,2,1,0:T(8,128)(2,1)} %get-tuple-element.1995) | copy-start | bytes 393220 | tf_op jit(solution)/shard_map/while
  352.8 6.0 copy-start.17
  368.2 4.9 copy-start.4
  373.0 9.1 %copy-start.11 = (bf16[2,2,64,256]{3,2,1,0:T(8,128)(2,1)S(1)}, bf16[2,2,64,256]{3,2,1,0:T(8,128)(2,1)}, u32[]{:S(2)}) copy-start(bf16[2,2,64,256]{3,2,1,0:T(8,128)(2,1)} %get-tuple-element.1995) | copy-start | bytes 393220 | tf_op jit(solution)/shard_map/while
  406.3 6.0 copy-start.17
  421.4 4.9 copy-start.5
  472.6 4.9 copy-start.5
  516.8 108.1 %copy-start.8 = (bf16[2,2,64,4,128]{4,3,2,1,0:T(4,128)(2,1)S(1)}, bf16[2,2,64,4,128]{4,3,2,1,0:T(4,128)(2,1)}, u32[]{:S(2)}) copy-start(bf16[2,2,64,4,128]{4,3,2,1,0:T(4,128)(2,1)} %get-tuple-element.1807) | copy-start | bytes 786436
  516.8 108.1 %copy-start.9 = (bf16[256,1,256]{2,0,1:T(8,128)(2,1)S(1)}, bf16[256,1,256]{2,0,1:T(8,128)(2,1)}, u32[]{:S(2)}) copy-start(bf16[256,1,256]{2,0,1:T(8,128)(2,1)} %get-tuple-element.1294) | copy-start | bytes 393220
  516.8 108.1 %copy-start.12 = (bf16[128,256]{1,0:T(8,128)(2,1)S(1)}, bf16[128,256]{1,0:T(8,128)(2,1)}, u32[]{:S(2)}) copy-start(bf16[128,256]{1,0:T(8,128)(2,1)} %get-tuple-element.1820) | copy-start | bytes 196612
  516.8 108.1 %copy-start.15 = (s32[1,4,40]{2,1,0:T(4,128)S(1)}, s32[1,4,40]{2,1,0:T(4,128)}, u32[]{:S(2)}) copy-start(s32[1,4,40]{2,1,0:T(4,128)} %get-tuple-element.1302) | copy-start | bytes 1924
  527.2 4.9 copy-start.6
  532.1 9.1 %copy-start.10 = (bf16[2,2,64,256]{3,2,1,0:T(8,128)(2,1)S(1)}, bf16[2,2,64,256]{3,2,1,0:T(8,128)(2,1)}, u32[]{:S(2)}) copy-start(bf16[2,2,64,256]{3,2,1,0:T(8,128)(2,1)} %get-tuple-element.1893) | copy-start | bytes 393220 | tf_op jit(solution)/shard_map/while
  580.7 4.9 copy-start.6
  585.6 9.1 %copy-start.10 = (bf16[2,2,64,256]{3,2,1,0:T(8,128)(2,1)S(1)}, bf16[2,2,64,256]{3,2,1,0:T(8,128)(2,1)}, u32[]{:S(2)}) copy-start(bf16[2,2,64,256]{3,2,1,0:T(8,128)(2,1)} %get-tuple-element.1893) | copy-start | bytes 393220 | tf_op jit(solution)/shard_map/while
  632.9 4.9 copy-start.7
  684.2 4.9 copy-start.7
  (12 other events, 44.5 us)
Sparse Core Ops, SparseCore 0:
  53.9 187.5 all-gather.2
